TPU v7x, 32 devices: a whole 2x2x4 slice. The times are simulated.
32 devices in a mesh: region: 4 (over y, x), col: 8 (over z, core).
Axes of the slice: x: 2, y: 2, z: 4, core: 2. Of those that a mesh axis runs over, the one named last changes fastest.
Arguments:
- jac: bfloat16 [256, 128], P(('region', 'col')), may hold values from -2 to 2
- dest: int32 [256, 2], P(('region', 'col')), may hold values from 0 to 3, all different within a row; in each aligned block of 8 rows (0 to 7, 8 to 15, ...) at most 6 rows name the same one
- near_pose: int32 [256, 2], P(('region', 'col')), may hold values from 0 to 255
- prior: float32 [8192], P('region'), may hold values from 0.5 to 8
Outputs:
- front_out: float32 [8192, 8192], P('region', 'col')
Inputs may be any that keep to these rules, and one draw needn't show every extreme that they name: `dest`: each row names two different regions; among the 8 rows of one device no region is named more than 6 times, and in some device's rows some region is named exactly 6 times.
All inputs are finite; a program needn't handle non-finite values.
Results may differ from a plain program's by a relative error of at most 0.00045.
Values may be sent and summed in bfloat16 or wider, within the bound.
No kernel may reach another device: no remote copies, remote signals or barrier semaphores. Data moves between devices by JAX's collectives and lax.ppermute only.
A program may use at most 320 MiB of HBM per device.

v0:
```python
import jax
import jax.numpy as jnp
from jax import lax
from jax.sharding import PartitionSpec as P

NB = 128
K_PANELS = 2


def broadcast(block, axis, owner):
    block = jnp.where(lax.axis_index(axis) == owner, block, jnp.zeros_like(block))
    return lax.psum(block, axis)


def placed(pose_pair, blocks, first_pose, pose_count):
    pose_grid = first_pose + jnp.arange(pose_count, dtype=jnp.int32)
    summed = jnp.zeros((blocks.shape[0], 8, pose_count, 8), jnp.float32)
    for endpoint in range(2):
        matches = (pose_pair[:, endpoint][:, None] == pose_grid[None, :]).astype(jnp.float32)
        summed = summed + matches[:, None, :, None] * blocks[:, endpoint][:, :, None, :]
    return summed.astype(jnp.bfloat16).reshape(blocks.shape[0] * 8, pose_count * 8)


def body(jac, dest, near_pose, prior):
    regions = lax.axis_size("region")
    columns = lax.axis_size("col")
    region_index = lax.axis_index("region")
    column_index = lax.axis_index("col")
    count_rows = jac.shape[0]
    row_block = prior.shape[0]
    front = row_block * regions
    col_block = front // columns
    region_poses = front // 8 // regions
    capacity = max(2, 3 * count_rows // regions)
    slots_out = regions * capacity
    targets = dest.reshape(-1)
    member = (targets[:, None] == jnp.arange(regions, dtype=jnp.int32)[None, :]).astype(jnp.int32)
    ranking = jnp.sum(jnp.cumsum(member, axis=0) * member, axis=1) - 1
    position = targets * capacity + ranking
    placing = (position[None, :] == jnp.arange(slots_out, dtype=jnp.int32)[:, None]).astype(
        jnp.bfloat16
    )
    copies = jnp.repeat(jac, 2, axis=0)
    labels = jnp.concatenate([near_pose // 64, near_pose % 64, dest], axis=1).astype(jnp.bfloat16)
    label_copies = jnp.repeat(labels, 2, axis=0)
    packed = (
        jnp.dot(placing, copies, preferred_element_type=jnp.float32)
        .astype(jnp.bfloat16)
        .reshape(regions, capacity, 128)
    )
    packed_labels = (
        jnp.dot(placing, label_copies, preferred_element_type=jnp.float32)
        .astype(jnp.bfloat16)
        .reshape(regions, capacity, 6)
    )
    arrived, arrived_labels = (
        lax.all_to_all(packed, "region", split_axis=0, concat_axis=0, tiled=True),
        lax.all_to_all(packed_labels, "region", split_axis=0, concat_axis=0, tiled=True),
    )
    piece_rows = lax.all_gather(arrived, "col", axis=0, tiled=True)
    piece_labels = lax.all_gather(arrived_labels, "col", axis=0, tiled=True)
    slot_count = piece_rows.shape[0] * piece_rows.shape[1]
    blocks = piece_rows.reshape(slot_count, 2, 8, 8).astype(jnp.float32)
    label_values = piece_labels.reshape(slot_count, 6).astype(jnp.int32)
    near_values = label_values[:, 0:2] * 64 + label_values[:, 2:4]
    pose_pair = label_values[:, 4:6] * region_poses + near_values
    own_rows = placed(pose_pair, blocks, region_index * region_poses, region_poses)
    own_cols = placed(pose_pair, blocks, column_index * (col_block // 8), col_block // 8)
    matrix = lax.dot_general(
        own_rows, own_cols, (((0,), (0,)), ((), ())), preferred_element_type=jnp.float32
    )
    row_global = region_index * row_block + jnp.arange(row_block, dtype=jnp.int32)
    col_global = column_index * col_block + jnp.arange(col_block, dtype=jnp.int32)
    matrix = matrix + jnp.where(row_global[:, None] == col_global[None, :], prior[:, None], 0.0)
    for panel_number in range(K_PANELS):
        low_edge = panel_number * NB
        high_edge = low_edge + NB
        owner_col = low_edge // col_block
        offset_col = low_edge - owner_col * col_block
        local_panel = lax.slice_in_dim(matrix, offset_col, offset_col + NB, axis=1)
        panel_part = broadcast(local_panel.astype(jnp.bfloat16), "col", owner_col).astype(
            local_panel.dtype
        )
        whole_panel = lax.all_gather(
            panel_part.astype(jnp.bfloat16), "region", axis=0, tiled=True
        ).astype(panel_part.dtype)
        diagonal = lax.slice_in_dim(whole_panel, low_edge, high_edge, axis=0)
        their_rows = lax.dynamic_slice_in_dim(
            whole_panel, column_index * col_block, col_block, axis=0
        )
        factor = jnp.tril(jnp.linalg.cholesky(diagonal))
        panel_cols = low_edge + jnp.arange(NB, dtype=jnp.int32)

        def finish(block_rows, global_rows):
            solved = jax.scipy.linalg.solve_triangular(factor, block_rows.T, lower=True).T
            keeping = global_rows[:, None] >= panel_cols[None, :]
            return jnp.where(keeping, solved, 0.0)

        mine = finish(panel_part, row_global)
        theirs = finish(their_rows, col_global)
        matrix = matrix - jnp.dot(mine, theirs.T, precision=lax.Precision.HIGHEST)
        with_panel = matrix.at[:, offset_col : offset_col + NB].set(mine)
        matrix = jnp.where(column_index == owner_col, with_panel, matrix)
        in_panel = (row_global >= low_edge) & (row_global < high_edge)
        right_side = col_global >= high_edge
        matrix = jnp.where(in_panel[:, None] & right_side[None, :], 0.0, matrix)
    return matrix


def solution(mesh):
    return jax.shard_map(
        body,
        mesh=mesh,
        in_specs=(
            P(("region", "col"), None),
            P(("region", "col"), None),
            P(("region", "col"), None),
            P("region"),
        ),
        out_specs=P("region", "col"),
        check_vma=False,
    )
```

profile of v0, /device:TPU:0, one launch (start us, length us, event | category | flops | bytes accessed | tf_op | source)
XLA Modules:
  0.0 640.7 jit_solution(2428502559729770655)
XLA Ops:
  10.1 5.2 all-to-all-start
  16.0 3.9 all-to-all-done
  19.9 3.2 all-to-all-start.1
  23.4 14.2 %all_gather.12 = bf16[32,6,6]{2,1,0:T(8,128)(2,1)S(1)} all-gather(bf16[4,6,6]{2,1,0:T(8,128)(2,1)S(1)} %copy.35), channel_id=1, replica_groups=mesh['region'=4,'col'=8] {'col'}, dimensions={0}, use_global_device_ids=true | all-gather | bytes 2592 | tf_op jit(solution)/shard_map/all_gather | solution.py:61
  38.9 14.0 %all_gather.13 = bf16[32,6,128]{2,1,0:T(8,128)(2,1)S(1)} all-gather(bf16[4,6,128]{2,1,0:T(8,128)(2,1)S(1)} %all-to-all-done.1), channel_id=1, replica_groups=mesh['region'=4,'col'=8] {'col'}, dimensions={0}, use_global_device_ids=true | all-gather | bytes 55296 | tf_op jit(solution)/shard_map/all_gather | solution.py:60
  53.9 43.1 %add_convert_fusion = bf16[192,8,256,8]{3,2,1,0:T(8,128)(2,1)} fusion(f32[192,8,8]{2,1,0:T(8,128)S(1)} %get-tuple-element.33, f32[192,256]{1,0:T(8,128)S(1)} %get-tuple-element.37, f32[192,8,8]{2,1,0:T(8,128)S(1)} %get-tuple-element.32, f32[192,256]{1,0:T(8,128)S(1)} %get-tuple-element.36), kind=kLoop, calls=%fused_computation | loop fusion | flops 12582912 | bytes 6782976 | tf_op jit(solution)/shard_map/convert_element_type | solution.py:21
  96.9 141.8 %convert_element_type.99 = bf16[1536,2048]{1,0:T(8,128)(2,1)} reshape(bf16[192,8,256,8]{3,2,1,0:T(8,128)(2,1)} %add_convert_fusion) | data formatting | bytes 12582912 | tf_op jit(solution)/shard_map/convert_element_type | solution.py:21
  238.7 23.6 %add_convert_fusion.1 = bf16[192,8,128,8]{3,2,1,0:T(8,128)(2,1)} fusion(f32[192,8,8]{2,1,0:T(8,128)S(1)} %get-tuple-element.33, f32[192,128]{1,0:T(8,128)S(1)} %copy-done.9, f32[192,8,8]{2,1,0:T(8,128)S(1)} %get-tuple-element.32, f32[192,128]{1,0:T(8,128)S(1)} %copy-done.8), kind=kLoop, calls=%fused_computation.1 | loop fusion | flops 6291456 | bytes 3440640 | tf_op jit(solution)/shard_map/convert_element_type | solution.py:21
  262.3 71.0 %convert_element_type.103 = bf16[1536,1024]{1,0:T(8,128)(2,1)S(1)} reshape(bf16[192,8,128,8]{3,2,1,0:T(8,128)(2,1)} %add_convert_fusion.1) | data formatting | bytes 6291456 | tf_op jit(solution)/shard_map/convert_element_type | solution.py:21
  333.3 9.5 %select_add_fusion = f32[2048,1024]{0,1:T(8,128)S(1)} fusion(f32[2048]{0:T(1024)S(1)} %copy-done.10, s32[2048]{0:T(1024)S(1)} %iota_add_fusion, s32[1024]{0:T(1024)S(1)} %iota_add_fusion.1, bf16[1536,2048]{1,0:T(8,128)(2,1)} %convert_element_type.99, bf16[1536,1024]{1,0:T(8,128)(2,1)S(1)} %convert_element_type.103), kind=kOutput, calls=%fused_computation.2 | convolution fusion | flops 6448742400 | bytes 17846272 | tf_op jit(solution)/shard_map/dot_general | solution.py:69
  342.8 3.4 copy-done.3
  347.1 58.0 %all-reduce.3.cloned.1.call-done = bf16[2048,128]{0,1:T(8,128)(2,1)} async-done(((bf16[2048,128]{0,1:T(8,128)(2,1)}), bf16[2048,128]{0,1:T(8,128)(2,1)}) %all-reduce.3.cloned.1.call-update) | async-done | bytes 524304 | tf_op jit(solution)/shard_map/psum | solution.py:12
  406.0 35.2 %all-gather.3.cloned.1.call-done = bf16[8192,128]{0,1:T(8,128)(2,1)} async-done(((bf16[2048,128]{0,1:T(8,128)(2,1)}), bf16[8192,128]{0,1:T(8,128)(2,1)}) %all-gather.3.cloned.1.call-update) | async-done | bytes 2097168 | tf_op jit(solution)/shard_map/all_gather | solution.py:84
  446.1 11.7 %cholesky.44 = f32[128,128]{1,0:T(8,128)S(1)} custom-call(f32[128,128]{1,0:T(8,128)S(1)} %fusion.25), custom_call_target="Cholesky" | custom-call | tf_op jit(solution)/shard_map/jit(cholesky)/cholesky | solution.py:91
  459.2 9.8 %custom-call.10 = f32[1,128,128]{1,2,0:T(8,128)S(1)} custom-call(f32[1,128,128]{2,1,0:T(8,128)S(1)} %fusion.18), custom_call_target="InvertDiagBlocksLowerTriangular" | custom-call | tf_op jit(solution)/shard_map/jit(_solve_triangular)/triangular_solve | solution.py:95
  471.8 9.4 %convolution_subtract_fusion.1 = f32[2048,1024]{0,1:T(8,128)S(1)} fusion(f32[2048,1024]{0,1:T(8,128)} %copy-done.3, f32[2048,128]{0,1:T(8,128)S(1)} %fusion.1, f32[1024,128]{0,1:T(8,128)S(1)} %fusion.3), kind=kOutput, calls=%fused_computation.6 | convolution fusion | flops 3223322624 | bytes 18350080 | tf_op jit(solution)/shard_map/dot_general | solution.py:101
  482.9 3.4 copy-done.2
  487.2 56.6 %all-reduce.5.cloned.1.call-done = bf16[2048,128]{0,1:T(8,128)(2,1)} async-done(((bf16[2048,128]{0,1:T(8,128)(2,1)}), bf16[2048,128]{0,1:T(8,128)(2,1)}) %all-reduce.5.cloned.1.call-update) | async-done | bytes 524304 | tf_op jit(solution)/shard_map/psum | solution.py:12
  544.6 35.3 %all-gather.5.cloned.1.call-done = bf16[8192,128]{0,1:T(8,128)(2,1)} async-done(((bf16[2048,128]{0,1:T(8,128)(2,1)}), bf16[8192,128]{0,1:T(8,128)(2,1)}) %all-gather.5.cloned.1.call-update) | async-done | bytes 2097168 | tf_op jit(solution)/shard_map/all_gather | solution.py:84
  584.7 11.7 %cholesky.55 = f32[128,128]{1,0:T(8,128)S(1)} custom-call(f32[128,128]{1,0:T(8,128)S(1)} %fusion.22), custom_call_target="Cholesky" | custom-call | tf_op jit(solution)/shard_map/jit(cholesky)/cholesky | solution.py:91
  597.8 9.8 %custom-call.12 = f32[1,128,128]{1,2,0:T(8,128)S(1)} custom-call(f32[1,128,128]{2,1,0:T(8,128)S(1)} %fusion.19), custom_call_target="InvertDiagBlocksLowerTriangular" | custom-call | tf_op jit(solution)/shard_map/jit(_solve_triangular)/triangular_solve | solution.py:95
  610.4 9.2 %convolution_subtract_fusion = f32[2048,1024]{0,1:T(8,128)S(1)} fusion(f32[2048,1024]{0,1:T(8,128)} %copy-done.2, f32[2048,128]{0,1:T(8,128)S(1)} %fusion, f32[1024,128]{0,1:T(8,128)S(1)} %fusion.2), kind=kOutput, calls=%fused_computation.5 | convolution fusion | flops 3223322624 | bytes 18350080 | tf_op jit(solution)/shard_map/dot_general | solution.py:101
  620.4 4.1 and_select_fusion.1
  624.5 9.2 %copy.43 = f32[2048,1024]{1,0:T(8,128)} copy(f32[2048,1024]{0,1:T(8,128)} %and_select_fusion.1) | data formatting | bytes 16777216 | tf_op jit(solution)/shard_map/jit(_where)/select_n | solution.py:106
  (91 shorter events, 30.6 us)
Async XLA Ops:
  6.5 8.7 %copy-start = (bf16[8,128]{1,0:T(8,128)(2,1)S(1)}, bf16[8,128]{1,0:T(8,128)(2,1)}, u32[]{:S(2)}) copy-start(bf16[8,128]{1,0:T(8,128)(2,1)} %param.13) | copy-start | bytes 6148
  10.1 9.9 %all-to-all-start = ((bf16[4,6,6]{1,2,0:T(8,128)(2,1)}), bf16[4,6,6]{1,2,0:T(8,128)(2,1)S(1)}, u32[]{:S(2)}, u32[]{:S(2)}) async-start(bf16[4,6,6]{1,2,0:T(8,128)(2,1)} %copy.34), calls=%async_computation | async-start | bytes 16384 | tf_op jit(solution)/shard_map/all_to_all | solution.py:58
  19.9 19.0 %all-to-all-start.1 = ((bf16[4,6,128]{2,1,0:T(8,128)(2,1)}), bf16[4,6,128]{2,1,0:T(8,128)(2,1)S(1)}, u32[]{:S(2)}, u32[]{:S(2)}) async-start(bf16[4,6,128]{2,1,0:T(8,128)(2,1)} %reshape.292), calls=%async_computation.1 | async-start | bytes 16384 | tf_op jit(solution)/shard_map/all_to_all | solution.py:57
  23.2 381.9 %all-reduce.3.cloned.1.call-start = ((), (), s32[]{:S(2)}) async-start(), calls=%async_computation.2 | async-start | bytes 1048576 | tf_op jit(solution)/shard_map/psum | solution.py:12
  96.9 141.8 %copy-start.8 = (f32[192,128]{1,0:T(8,128)S(1)}, f32[192,128]{1,0:T(8,128)}, u32[]{:S(2)}) copy-start(f32[192,128]{1,0:T(8,128)} %get-tuple-element.40) | copy-start | bytes 294916
  96.9 141.8 %copy-start.9 = (f32[192,128]{1,0:T(8,128)S(1)}, f32[192,128]{1,0:T(8,128)}, u32[]{:S(2)}) copy-start(f32[192,128]{1,0:T(8,128)} %get-tuple-element.41) | copy-start | bytes 294916
  262.3 71.0 %copy-start.10 = (f32[2048]{0:T(1024)S(1)}, f32[2048]{0:T(1024)}, u32[]{:S(2)}) copy-start(f32[2048]{0:T(1024)} %param.16) | copy-start | bytes 24580
  342.8 3.4 copy-start.3
  347.1 94.2 %all-gather.3.cloned.1.call-start = ((), (), s32[]{:S(2)}) async-start(), calls=%async_computation.3 | async-start | bytes 2621440 | tf_op jit(solution)/shard_map/all_gather | solution.py:84
  405.1 65.5 %copy-start.6 = (bf16[2048,128]{0,1:T(8,128)(2,1)S(1)}, bf16[2048,128]{0,1:T(8,128)(2,1)}, u32[]{:S(2)}) copy-start(bf16[2048,128]{0,1:T(8,128)(2,1)} %all-reduce.3.cloned.1.call-done) | copy-start | bytes 1572868
  405.2 138.7 %all-reduce.5.cloned.1.call-start = ((), (), s32[]{:S(2)}) async-start(), calls=%async_computation.4 | async-start | bytes 1048576 | tf_op jit(solution)/shard_map/psum | solution.py:12
  444.1 1.9 copy-start.5
  482.9 3.4 copy-start.2
  487.2 92.7 %all-gather.5.cloned.1.call-start = ((), (), s32[]{:S(2)}) async-start(), calls=%async_computation.5 | async-start | bytes 2621440 | tf_op jit(solution)/shard_map/all_gather | solution.py:84
  543.9 65.4 %copy-start.7 = (bf16[2048,128]{0,1:T(8,128)(2,1)S(1)}, bf16[2048,128]{0,1:T(8,128)(2,1)}, u32[]{:S(2)}) copy-start(bf16[2048,128]{0,1:T(8,128)(2,1)} %all-reduce.5.cloned.1.call-done) | copy-start | bytes 1572868
  582.7 1.9 copy-start.4
  620.4 13.4 %copy-start.1 = (bf16[8,128]{1,0:T(8,128)(2,1)S(1)}, bf16[8,128]{1,0:T(8,128)(2,1)}, u32[]{:S(2)}) copy-start(bf16[8,128]{1,0:T(8,128)(2,1)} %param.13) | copy-start | bytes 6148
Sparse Core Ops, SparseCore 0:
  347.2 57.9 all-reduce.2
  407.0 34.2 all-gather.2
  487.3 56.5 all-reduce.4
  545.6 34.2 all-gather.4
where the time goes:
time: 649 us; the launch traced here: 641 us
  local copies, waits for them, and re-layouts  238 us (37%)
  waiting for transfers between devices  189 us (29%)
  other arithmetic  129 us (20%)
  matrix products  33.8 us (5%)
  blocking collectives  28.2 us (4%)
  between operations  13.8 us (2%)
  starting transfers between devices  8.78 us (1%)
    convert_element_type x2, local copies, waits for them, and re-layouts, placed(): summed.astype(jnp.bfloat16).reshape(blocks.shape[0] * 8, pose_count * 8)  213 us
    psum x2, waiting for transfers between devices, broadcast(): return lax.psum(block, axis)  115 us
    all_gather x2, waiting for transfers between devices, body(): lax.all_gather(panel_part.astype(jnp.bfloat16), 'region', axis=0, tiled=T...  70.5 us
    convert_element_type x2, other arithmetic, placed(): summed.astype(jnp.bfloat16).reshape(blocks.shape[0] * 8, pose_count * 8)  66.7 us
    another operation x6, other arithmetic, body(): factor = jnp.tril(jnp.linalg.cholesky(diagonal))  24.9 us
    another operation x4, other arithmetic, finish(): jax.scipy.linalg.solve_triangular(factor, block_rows.T, lower=True)  20.9 us
    dot_general x2, matrix products, body(): matrix = matrix - jnp.dot(mine, theirs.T, precision=lax.Precision.HIGHEST)  18.5 us
    all_gather x1, blocking collectives, body(): piece_labels = lax.all_gather(arrived_labels, 'col', axis=0, tiled=True)  14.2 us
  transfers between devices with their start and end apart: 6, of which 5 were waited for; matrix products, arithmetic and copies ran while one was open for 1% of the time, Pallas kernels for 0%

commit v1 on v0

--- a/solution.py
+++ b/solution.py
@@ -9,7 +9,7 @@
 
 def broadcast(block, axis, owner):
     block = jnp.where(lax.axis_index(axis) == owner, block, jnp.zeros_like(block))
-    return lax.psum(block, axis)
+    return jnp.sum(lax.all_gather(block, axis), axis=0)
 
 
 def placed(pose_pair, blocks, first_pose, pose_count):

time: 649 us -> 625 us (0.963)
  waiting for transfers between devices: 189 us -> 156 us
  other arithmetic: 129 us -> 145 us
  local copies, waits for them, and re-layouts: 238 us -> 231 us
    psum x2 -> x0, waiting for transfers between devices: 115 us -> none  [broadcast(): return lax.psum(block, axis)]
    all_gather x0 -> x2, waiting for transfers between devices: none -> 95.3 us  [broadcast(): return jnp.sum(lax.all_gather(block, axis), axis=0)]
    all_gather x2, waiting for transfers between devices: 70.5 us -> 57.1 us  [body(): lax.all_gather(panel_part.astype(jnp.bfloat16), 'region', axis=0, tiled=T...]
    another operation x4, other arithmetic: 2.65 us -> 12.5 us
    select_n x1 -> x0, local copies, waits for them, and re-layouts: 9.24 us -> none  [body(): matrix = jnp.where(in_panel[:, None] & right_side[None, :], 0.0, matrix)]
  transfers between devices with their start and end apart: 6 -> 6, of which waited for: 5 -> 5; matrix products, arithmetic and copies ran while one was open for 1% -> 2% of each run, Pallas kernels for 0% -> 0%
where the time goes in v1:
time: 625 us; the launch traced here: 616 us
  local copies, waits for them, and re-layouts  231 us (37%)
  waiting for transfers between devices  156 us (25%)
  other arithmetic  145 us (23%)
  matrix products  32.9 us (5%)
  blocking collectives  28.2 us (5%)
  between operations  13.8 us (2%)
  starting transfers between devices  8.61 us (1%)
    convert_element_type x2, local copies, waits for them, and re-layouts, placed(): summed.astype(jnp.bfloat16).reshape(blocks.shape[0] * 8, pose_count * 8)  213 us
    all_gather x2, waiting for transfers between devices, broadcast(): return jnp.sum(lax.all_gather(block, axis), axis=0)  95.3 us
    convert_element_type x2, other arithmetic, placed(): summed.astype(jnp.bfloat16).reshape(blocks.shape[0] * 8, pose_count * 8)  66.7 us
    all_gather x2, waiting for transfers between devices, body(): lax.all_gather(panel_part.astype(jnp.bfloat16), 'region', axis=0, tiled=T...  57.1 us
    another operation x6, other arithmetic, body(): factor = jnp.tril(jnp.linalg.cholesky(diagonal))  24.8 us
    another operation x4, other arithmetic, finish(): jax.scipy.linalg.solve_triangular(factor, block_rows.T, lower=True)  20.8 us
    dot_general x2, matrix products, body(): matrix = matrix - jnp.dot(mine, theirs.T, precision=lax.Precision.HIGHEST)  18.2 us
    all_gather x1, blocking collectives, body(): piece_labels = lax.all_gather(arrived_labels, 'col', axis=0, tiled=True)  14.2 us
  transfers between devices with their start and end apart: 6, of which 5 were waited for; matrix products, arithmetic and copies ran while one was open for 2% of the time, Pallas kernels for 0%

profile of v1, /device:TPU:0, one launch (start us, length us, event | category | flops | bytes accessed | tf_op | source)
XLA Modules:
  0.0 615.6 jit_solution(17835676417935256905)
XLA Ops:
  10.1 5.2 all-to-all-start
  16.0 3.9 all-to-all-done
  19.9 3.2 all-to-all-start.1
  23.4 14.2 %all_gather.24 = bf16[32,6,6]{2,1,0:T(8,128)(2,1)S(1)} all-gather(bf16[4,6,6]{2,1,0:T(8,128)(2,1)S(1)} %copy.31), channel_id=1, replica_groups=mesh['region'=4,'col'=8] {'col'}, dimensions={0}, use_global_device_ids=true | all-gather | bytes 2592 | tf_op jit(solution)/shard_map/all_gather | solution.py:61
  38.9 14.0 %all_gather.25 = bf16[32,6,128]{2,1,0:T(8,128)(2,1)S(1)} all-gather(bf16[4,6,128]{2,1,0:T(8,128)(2,1)S(1)} %all-to-all-done.1), channel_id=1, replica_groups=mesh['region'=4,'col'=8] {'col'}, dimensions={0}, use_global_device_ids=true | all-gather | bytes 55296 | tf_op jit(solution)/shard_map/all_gather | solution.py:60
  53.8 43.1 %add_convert_fusion = bf16[192,8,256,8]{3,2,1,0:T(8,128)(2,1)} fusion(f32[192,8,8]{2,1,0:T(8,128)S(1)} %get-tuple-element.33, f32[192,256]{1,0:T(8,128)S(1)} %get-tuple-element.37, f32[192,8,8]{2,1,0:T(8,128)S(1)} %get-tuple-element.32, f32[192,256]{1,0:T(8,128)S(1)} %get-tuple-element.36), kind=kLoop, calls=%fused_computation | loop fusion | flops 12582912 | bytes 6782976 | tf_op jit(solution)/shard_map/convert_element_type | solution.py:21
  96.9 141.8 %convert_element_type.115 = bf16[1536,2048]{1,0:T(8,128)(2,1)} reshape(bf16[192,8,256,8]{3,2,1,0:T(8,128)(2,1)} %add_convert_fusion) | data formatting | bytes 12582912 | tf_op jit(solution)/shard_map/convert_element_type | solution.py:21
  238.7 23.6 %add_convert_fusion.1 = bf16[192,8,128,8]{3,2,1,0:T(8,128)(2,1)} fusion(f32[192,8,8]{2,1,0:T(8,128)S(1)} %get-tuple-element.33, f32[192,128]{1,0:T(8,128)S(1)} %copy-done.7, f32[192,8,8]{2,1,0:T(8,128)S(1)} %get-tuple-element.32, f32[192,128]{1,0:T(8,128)S(1)} %copy-done.6), kind=kLoop, calls=%fused_computation.1 | loop fusion | flops 6291456 | bytes 3440640 | tf_op jit(solution)/shard_map/convert_element_type | solution.py:21
  262.3 71.0 %convert_element_type.119 = bf16[1536,1024]{1,0:T(8,128)(2,1)S(1)} reshape(bf16[192,8,128,8]{3,2,1,0:T(8,128)(2,1)} %add_convert_fusion.1) | data formatting | bytes 6291456 | tf_op jit(solution)/shard_map/convert_element_type | solution.py:21
  333.3 9.1 %select_add_fusion = f32[2048,1024]{1,0:T(8,128)S(1)} fusion(f32[2048]{0:T(1024)S(1)} %copy-done.8, s32[1024]{0:T(1024)S(1)} %iota_add_fusion.1, s32[2048]{0:T(1024)S(1)} %iota_add_fusion, bf16[1536,2048]{1,0:T(8,128)(2,1)} %convert_element_type.115, bf16[1536,1024]{1,0:T(8,128)(2,1)S(1)} %convert_element_type.119), kind=kOutput, calls=%fused_computation.2 | convolution fusion | flops 6448742400 | bytes 17846272 | tf_op jit(solution)/shard_map/dot_general | solution.py:69
  342.4 3.4 copy-done.3
  346.8 48.4 %all-gather.11.cloned.1.call-done = bf16[16384,128]{1,0:T(8,128)(2,1)} async-done(((bf16[2048,128]{1,0:T(8,128)(2,1)}), bf16[16384,128]{1,0:T(8,128)(2,1)}) %all-gather.11.cloned.1.call-update) | async-done | bytes 4194320 | tf_op jit(solution)/shard_map/all_gather | solution.py:12
  399.3 10.2 %compare_reduce_fusion.3 = pred[]{:T(512)} fusion(), kind=kLoop, calls=%fused_computation.83 | loop fusion | flops 5 | bytes 1 | tf_op jit(solution)/shard_map/reduce.6
  409.5 23.9 %all-gather.7.cloned.1.call-done = bf16[8192,128]{0,1:T(8,128)(2,1)} async-done(((bf16[2048,128]{0,1:T(8,128)(2,1)}), bf16[8192,128]{0,1:T(8,128)(2,1)}) %all-gather.7.cloned.1.call-update) | async-done | bytes 2097168 | tf_op jit(solution)/shard_map/all_gather | solution.py:84
  438.2 11.7 %cholesky.44 = f32[128,128]{1,0:T(8,128)S(1)} custom-call(f32[128,128]{1,0:T(8,128)S(1)} %fusion.25), custom_call_target="Cholesky" | custom-call | tf_op jit(solution)/shard_map/jit(cholesky)/cholesky | solution.py:91
  451.2 9.8 %custom-call.10 = f32[1,128,128]{1,2,0:T(8,128)S(1)} custom-call(f32[1,128,128]{2,1,0:T(8,128)S(1)} %fusion.18), custom_call_target="InvertDiagBlocksLowerTriangular" | custom-call | tf_op jit(solution)/shard_map/jit(_solve_triangular)/triangular_solve | solution.py:95
  463.7 9.1 %convolution_subtract_fusion.1 = f32[2048,1024]{1,0:T(8,128)S(1)} fusion(f32[2048,1024]{1,0:T(8,128)} %copy-done.3, f32[2048,128]{1,0:T(8,128)S(1)} %fusion.1, f32[1024,128]{0,1:T(8,128)S(1)} %fusion.3), kind=kOutput, calls=%fused_computation.6 | convolution fusion | flops 3223322624 | bytes 18350080 | tf_op jit(solution)/shard_map/dot_general | solution.py:101
  474.8 3.4 copy-done.2
  479.2 47.0 %all-gather.13.cloned.1.call-done = bf16[16384,128]{1,0:T(8,128)(2,1)} async-done(((bf16[2048,128]{1,0:T(8,128)(2,1)}), bf16[16384,128]{1,0:T(8,128)(2,1)}) %all-gather.13.cloned.1.call-update) | async-done | bytes 4194320 | tf_op jit(solution)/shard_map/all_gather | solution.py:12
  531.2 33.2 %all-gather.9.cloned.1.call-done = bf16[8192,128]{0,1:T(8,128)(2,1)} async-done(((bf16[2048,128]{0,1:T(8,128)(2,1)}), bf16[8192,128]{0,1:T(8,128)(2,1)}) %all-gather.9.cloned.1.call-update) | async-done | bytes 2097168 | tf_op jit(solution)/shard_map/all_gather | solution.py:84
  569.3 11.7 %cholesky.55 = f32[128,128]{1,0:T(8,128)S(1)} custom-call(f32[128,128]{1,0:T(8,128)S(1)} %fusion.22), custom_call_target="Cholesky" | custom-call | tf_op jit(solution)/shard_map/jit(cholesky)/cholesky | solution.py:91
  582.2 9.8 %custom-call.12 = f32[1,128,128]{1,2,0:T(8,128)S(1)} custom-call(f32[1,128,128]{2,1,0:T(8,128)S(1)} %fusion.19), custom_call_target="InvertDiagBlocksLowerTriangular" | custom-call | tf_op jit(solution)/shard_map/jit(_solve_triangular)/triangular_solve | solution.py:95
  594.7 9.1 %convolution_subtract_fusion = f32[2048,1024]{1,0:T(8,128)S(1)} fusion(f32[2048,1024]{1,0:T(8,128)} %copy-done.2, f32[2048,128]{1,0:T(8,128)S(1)} %fusion, f32[1024,128]{0,1:T(8,128)S(1)} %fusion.2), kind=kOutput, calls=%fused_computation.5 | convolution fusion | flops 3223322624 | bytes 18350080 | tf_op jit(solution)/shard_map/dot_general | solution.py:101
  604.8 3.9 and_select_fusion.1
  (89 shorter events, 38.3 us)
Async XLA Ops:
  6.5 8.7 %copy-start = (bf16[8,128]{1,0:T(8,128)(2,1)S(1)}, bf16[8,128]{1,0:T(8,128)(2,1)}, u32[]{:S(2)}) copy-start(bf16[8,128]{1,0:T(8,128)(2,1)} %param.13) | copy-start | bytes 6148
  10.1 9.9 %all-to-all-start = ((bf16[4,6,6]{1,2,0:T(8,128)(2,1)}), bf16[4,6,6]{1,2,0:T(8,128)(2,1)S(1)}, u32[]{:S(2)}, u32[]{:S(2)}) async-start(bf16[4,6,6]{1,2,0:T(8,128)(2,1)} %copy.30), calls=%async_computation | async-start | bytes 16384 | tf_op jit(solution)/shard_map/all_to_all | solution.py:58
  19.9 19.0 %all-to-all-start.1 = ((bf16[4,6,128]{2,1,0:T(8,128)(2,1)}), bf16[4,6,128]{2,1,0:T(8,128)(2,1)S(1)}, u32[]{:S(2)}, u32[]{:S(2)}) async-start(bf16[4,6,128]{2,1,0:T(8,128)(2,1)} %reshape.292), calls=%async_computation.1 | async-start | bytes 16384 | tf_op jit(solution)/shard_map/all_to_all | solution.py:57
  23.2 372.0 %all-gather.11.cloned.1.call-start = ((), (), s32[]{:S(2)}) async-start(), calls=%async_computation.4 | async-start | bytes 4718592 | tf_op jit(solution)/shard_map/all_gather | solution.py:12
  96.9 141.8 %copy-start.6 = (f32[192,128]{1,0:T(8,128)S(1)}, f32[192,128]{1,0:T(8,128)}, u32[]{:S(2)}) copy-start(f32[192,128]{1,0:T(8,128)} %get-tuple-element.40) | copy-start | bytes 294916
  96.9 141.8 %copy-start.7 = (f32[192,128]{1,0:T(8,128)S(1)}, f32[192,128]{1,0:T(8,128)}, u32[]{:S(2)}) copy-start(f32[192,128]{1,0:T(8,128)} %get-tuple-element.41) | copy-start | bytes 294916
  262.3 71.0 %copy-start.8 = (f32[2048]{0:T(1024)S(1)}, f32[2048]{0:T(1024)}, u32[]{:S(2)}) copy-start(f32[2048]{0:T(1024)} %param.16) | copy-start | bytes 24580
  342.4 3.4 copy-start.3
  346.8 86.7 %all-gather.7.cloned.1.call-start = ((), (), s32[]{:S(2)}) async-start(), calls=%async_computation.2 | async-start | bytes 2621440 | tf_op jit(solution)/shard_map/all_gather | solution.py:84
  399.3 126.9 %all-gather.13.cloned.1.call-start = ((), (), s32[]{:S(2)}) async-start(), calls=%async_computation.5 | async-start | bytes 4718592 | tf_op jit(solution)/shard_map/all_gather | solution.py:12
  436.3 1.9 copy-start.5
  474.8 3.4 copy-start.2
  479.2 85.3 %all-gather.9.cloned.1.call-start = ((), (), s32[]{:S(2)}) async-start(), calls=%async_computation.3 | async-start | bytes 2621440 | tf_op jit(solution)/shard_map/all_gather | solution.py:84
  567.3 1.9 copy-start.4
  604.8 3.9 copy-start.1
Sparse Core Ops, SparseCore 0:
  346.9 48.2 all-gather.10
  399.4 33.9 all-gather.6
  479.3 46.8 all-gather.12
  530.4 33.9 all-gather.8
